TPU v7x, 32 devices: a whole 2x2x4 slice. The times are simulated.
32 devices in a mesh: fsdp: 8 (over y, x, core), tp: 4 (over z).
Axes of the slice: x: 2, y: 2, z: 4, core: 2. Of those that a mesh axis runs over, the one named last changes fastest.
Arguments:
- inputs: bfloat16 [32, 448, 768], P(('fsdp', 'tp')), may hold values from -6 to 6
- encoder: bfloat16 [32, 1500, 768], P('fsdp', 'tp'), may hold values from -6 to 6
- lengths: int32 [32], P('fsdp'), may hold values from 56 to 448, as said below
- self_qkv: bfloat16 [3, 768, 768], P(None, 'fsdp', 'tp'), may hold values from -0.21875 to 0.21875
- self_out: bfloat16 [768, 768], P('tp', 'fsdp'), may hold values from -0.875 to 0.875
- cross_q: bfloat16 [768, 768], P('fsdp', 'tp'), may hold values from -0.21875 to 0.21875
- cross_kv: bfloat16 [2, 768, 768], P(None, 'fsdp', 'tp'), may hold values from -0.21875 to 0.21875
- cross_out: bfloat16 [768, 768], P('tp', 'fsdp'), may hold values from -1.25 to 1.25
- fc_in: bfloat16 [768, 3072], P('fsdp', 'tp'), may hold values from -0.21875 to 0.21875
- fc_out: bfloat16 [3072, 768], P('tp', 'fsdp'), may hold values from -0.109375 to 0.109375
- norm_gain: float32 [4, 768], P(None, ('fsdp', 'tp')), may hold values from 0.5 to 1.5
- norm_bias: float32 [4, 768], P(None, ('fsdp', 'tp')), may hold values from -4 to 4
- proj_bias: float32 [7, 768], P(None, ('fsdp', 'tp')), may hold values from -4 to 4
- fc_in_bias: float32 [3072], P(('fsdp', 'tp')), may hold values from -4 to 4
- cotangent: bfloat16 [32, 448, 768], P(('fsdp', 'tp')), may hold values from -6 to 6
Outputs:
- layer_out: bfloat16 [32, 448, 768], P(('fsdp', 'tp'))
- grad_inputs: float32 [32, 448, 768], P(('fsdp', 'tp'))
- grad_encoder: float32 [32, 1500, 768], P('fsdp', 'tp')
- grad_self_qkv: float32 [3, 768, 768], P(None, 'fsdp', 'tp')
- grad_self_out: float32 [768, 768], P('tp', 'fsdp')
- grad_cross_q: float32 [768, 768], P('fsdp', 'tp')
- grad_cross_kv: float32 [2, 768, 768], P(None, 'fsdp', 'tp')
- grad_cross_out: float32 [768, 768], P('tp', 'fsdp')
- grad_fc_in: float32 [768, 3072], P('fsdp', 'tp')
- grad_fc_out: float32 [3072, 768], P('tp', 'fsdp')
- grad_norm_gain: float32 [4, 768], P(None, ('fsdp', 'tp'))
- grad_norm_bias: float32 [4, 768], P(None, ('fsdp', 'tp'))
- grad_proj_bias: float32 [7, 768], P(None, ('fsdp', 'tp'))
- grad_fc_in_bias: float32 [3072], P(('fsdp', 'tp'))
Inputs may be any that keep to these rules, and one draw needn't show every extreme that they name: `lengths`: valid tokens of each sequence; later positions are padding and never serve as keys.
All inputs are finite; a program needn't handle non-finite values.
Results may differ from a plain program's by a relative error of at most 0.035.
Values may be sent and summed in bfloat16 or wider, within the bound.
No kernel may reach another device: no remote copies, remote signals or barrier semaphores. Data moves between devices by JAX's collectives and lax.ppermute only.
A program may use at most 192 MiB of HBM per device.

v0:
```python
import jax
import jax.numpy as jnp
from jax import lax
from jax.sharding import PartitionSpec as P

HD = 64
EPSILON = 1e-05
NEGATIVE = -1e30


def normalize(row_block, gain_row, shift_row):
    center = row_block - jnp.mean(row_block, -1, keepdims=True)
    inverse = lax.rsqrt(jnp.mean(center * center, -1, keepdims=True) + EPSILON)
    unit_rows = center * inverse
    return (unit_rows * gain_row + shift_row, unit_rows, inverse)


def norm_back(grad_rows, unit_rows, inverse, gain_row):
    scaled = grad_rows * gain_row
    return inverse * (
        scaled
        - jnp.mean(scaled, -1, keepdims=True)
        - unit_rows * jnp.mean(scaled * unit_rows, -1, keepdims=True)
    )


def matmul(left_side, right_side):
    return jnp.dot(left_side, right_side, preferred_element_type=jnp.float32)


def transposed(left_side, right_side):
    return lax.dot_general(
        left_side, right_side, (((0,), (0,)), ((), ())), preferred_element_type=jnp.float32
    )


def against(left_side, right_side):
    return lax.dot_general(
        left_side, right_side, (((1,), (1,)), ((), ())), preferred_element_type=jnp.float32
    )


def exact_gelu(values):
    return jax.nn.gelu(values, approximate=False)


def row_sum(values):
    return jnp.sum(values.reshape(-1, values.shape[-1]), 0)


def attend_forward(query_seq, key_seq, value_seq, allowed):
    scores = jnp.einsum("qhd,khd->hqk", query_seq, key_seq, preferred_element_type=jnp.float32)
    if allowed is not None:
        scores = jnp.where(allowed[None], scores, NEGATIVE)
    highest = jnp.max(scores, -1, keepdims=True)
    shifted = jnp.exp(scores - highest)
    total = jnp.sum(shifted, -1, keepdims=True)
    weights = (shifted / total).astype(jnp.bfloat16)
    output = jnp.einsum("hqk,khd->qhd", weights, value_seq, preferred_element_type=jnp.float32)
    return (output, highest + jnp.log(total))


def attend_backward(query_seq, key_seq, value_seq, grad_out, log_total, allowed):
    scores = jnp.einsum("qhd,khd->hqk", query_seq, key_seq, preferred_element_type=jnp.float32)
    if allowed is not None:
        scores = jnp.where(allowed[None], scores, NEGATIVE)
    probs = jnp.exp(scores - log_total)
    grad_probs = jnp.einsum("qhd,khd->hqk", grad_out, value_seq, preferred_element_type=jnp.float32)
    grad_scores = (probs * (grad_probs - jnp.sum(probs * grad_probs, -1, keepdims=True))).astype(
        jnp.bfloat16
    )
    grad_query = jnp.einsum(
        "hqk,khd->qhd", grad_scores, key_seq, preferred_element_type=jnp.float32
    ).astype(jnp.bfloat16)
    grad_key = jnp.einsum(
        "hqk,qhd->khd", grad_scores, query_seq, preferred_element_type=jnp.float32
    ).astype(jnp.bfloat16)
    grad_value = jnp.einsum(
        "hqk,qhd->khd", probs.astype(jnp.bfloat16), grad_out, preferred_element_type=jnp.float32
    ).astype(jnp.bfloat16)
    return (grad_query, grad_key, grad_value)


def local(
    inputs,
    encoder,
    lengths,
    self_qkv,
    self_out,
    cross_q,
    cross_kv,
    cross_out,
    fc_in,
    fc_out,
    norm_gain,
    norm_bias,
    proj_bias,
    fc_in_bias,
    cotangent,
):
    tp_count = lax.axis_size("tp")
    tp_place = lax.axis_index("tp")
    local_seqs, seq_len, width_all = inputs.shape
    group_seqs = local_seqs * tp_count
    group_rows = group_seqs * seq_len
    head_width = width_all // tp_count
    local_heads = head_width // HD
    ff_width = fc_in.shape[1]
    own_frames = encoder.shape[1]
    frames_all = own_frames * tp_count
    head_scale = HD ** (-0.5)
    w_qkv, w_self_out, w_cross_q, w_cross_kv, w_cross_out, w_fc_in, w_fc_out = (
        lax.all_gather(self_qkv, "fsdp", axis=1, tiled=True),
        lax.all_gather(self_out, "fsdp", axis=1, tiled=True),
        lax.all_gather(cross_q, "fsdp", axis=0, tiled=True),
        lax.all_gather(cross_kv, "fsdp", axis=1, tiled=True),
        lax.all_gather(cross_out, "fsdp", axis=1, tiled=True),
        lax.all_gather(fc_in, "fsdp", axis=0, tiled=True),
        lax.all_gather(fc_out, "fsdp", axis=1, tiled=True),
    )
    gains, shifts, biases, fc_bias_all = (
        lax.all_gather(norm_gain, ("fsdp", "tp"), axis=1, tiled=True),
        lax.all_gather(norm_bias, ("fsdp", "tp"), axis=1, tiled=True),
        lax.all_gather(proj_bias, ("fsdp", "tp"), axis=1, tiled=True),
        lax.all_gather(fc_in_bias, ("fsdp", "tp"), axis=0, tiled=True),
    )
    head_start = tp_place * head_width
    ff_start = tp_place * ff_width

    def column(vector):
        return lax.dynamic_slice_in_dim(vector, head_start, head_width)

    def placed(vector):
        return lax.dynamic_update_slice_in_dim(
            jnp.zeros((width_all,), jnp.float32), vector, head_start, 0
        )

    fc_bias = lax.dynamic_slice_in_dim(fc_bias_all, ff_start, ff_width)

    def gather_rows(normed):
        whole = lax.all_gather(normed.astype(jnp.bfloat16), "tp", axis=0, tiled=True)
        return whole.reshape(group_rows, width_all)

    def scatter_rows(partial_out):
        return lax.psum_scatter(
            partial_out.reshape(group_seqs, seq_len, width_all).astype(jnp.bfloat16),
            "tp",
            scatter_dimension=0,
            tiled=True,
        ).astype(jnp.float32)

    def gather_grads(grad_rows):
        whole = lax.all_gather(grad_rows, "tp", axis=0, tiled=True)
        return whole.reshape(group_rows, width_all)

    def scatter_grads(partial_grad):
        return lax.psum_scatter(
            partial_grad.reshape(group_seqs, seq_len, width_all).astype(jnp.bfloat16),
            "tp",
            scatter_dimension=0,
            tiled=True,
        ).astype(jnp.float32)

    def split_heads(flat):
        return flat.reshape(group_seqs, seq_len, local_heads, HD)

    positions = jnp.arange(seq_len)

    def self_mask(length):
        return (positions[None, :] <= positions[:, None]) & (positions[None, :] < length)

    inputs_f = inputs.astype(jnp.float32)
    normed_one, unit_one, inv_one = normalize(inputs_f, gains[0], shifts[0])
    rows_one = gather_rows(normed_one)
    query_one = ((matmul(rows_one, w_qkv[0]) + column(biases[0])) * head_scale).astype(jnp.bfloat16)
    key_one = matmul(rows_one, w_qkv[1]).astype(jnp.bfloat16)
    value_one = (matmul(rows_one, w_qkv[2]) + column(biases[1])).astype(jnp.bfloat16)

    def self_forward(item):
        return attend_forward(item[0], item[1], item[2], self_mask(item[3]))

    attended_one, total_one = lax.map(
        self_forward,
        (split_heads(query_one), split_heads(key_one), split_heads(value_one), lengths),
    )
    mixed_one = attended_one.astype(jnp.bfloat16).reshape(group_rows, head_width)
    first = inputs_f + scatter_rows(matmul(mixed_one, w_self_out)) + biases[2]
    normed_two, unit_two, inv_two = normalize(first, gains[1], shifts[1])
    rows_two = gather_rows(normed_two)
    query_two = ((matmul(rows_two, w_cross_q) + column(biases[3])) * head_scale).astype(
        jnp.bfloat16
    )
    head_shape = (group_seqs, frames_all, local_heads, HD)
    frames = lax.all_gather(encoder, "tp", axis=1, tiled=True)
    flat_frames = frames.reshape(group_seqs * frames_all, width_all)
    key_two = matmul(flat_frames, w_cross_kv[0]).astype(jnp.bfloat16).reshape(head_shape)
    value_two = (
        (matmul(flat_frames, w_cross_kv[1]) + column(biases[4]))
        .astype(jnp.bfloat16)
        .reshape(head_shape)
    )

    def cross_forward(item):
        return attend_forward(item[0], item[1], item[2], None)

    attended_two, total_two = lax.map(cross_forward, (split_heads(query_two), key_two, value_two))
    mixed_two = attended_two.astype(jnp.bfloat16).reshape(group_rows, head_width)
    second = first + scatter_rows(matmul(mixed_two, w_cross_out)) + biases[5]
    normed_three, unit_three, inv_three = normalize(second, gains[2], shifts[2])
    rows_three = gather_rows(normed_three)
    before = matmul(rows_three, w_fc_in) + fc_bias
    hidden = exact_gelu(before).astype(jnp.bfloat16)
    third = second + scatter_rows(matmul(hidden, w_fc_out)) + biases[6]
    result, unit_four, inv_four = normalize(third, gains[3], shifts[3])
    grad_result = cotangent.astype(jnp.float32)
    gain_four = row_sum(grad_result * unit_four)
    shift_four = row_sum(grad_result)
    grad_third = norm_back(grad_result, unit_four, inv_four, gains[3])
    branch_three = grad_third.astype(jnp.bfloat16)
    bias_six = row_sum(branch_three.astype(jnp.float32))
    down_three = gather_grads(branch_three)
    grad_hidden = against(down_three, w_fc_out)
    grad_fc_out = transposed(hidden, down_three)
    grad_before = jax.vjp(exact_gelu, before)[1](grad_hidden)[0].astype(jnp.bfloat16)
    grad_fc_bias = jnp.sum(grad_before.astype(jnp.float32), 0)
    grad_fc_in = transposed(rows_three, grad_before)
    grad_normed_three = scatter_grads(against(grad_before, w_fc_in))
    gain_three = row_sum(grad_normed_three * unit_three)
    shift_three = row_sum(grad_normed_three)
    grad_second = grad_third + norm_back(grad_normed_three, unit_three, inv_three, gains[2])
    branch_two = grad_second.astype(jnp.bfloat16)
    bias_five = row_sum(branch_two.astype(jnp.float32))
    down_two = gather_grads(branch_two)
    grad_mixed_two = against(down_two, w_cross_out).astype(jnp.bfloat16)
    grad_cross_out = transposed(mixed_two, down_two)

    def cross_backward(item):
        return attend_backward(item[0], item[1], item[2], item[3], item[4], None)

    grad_query_two, grad_key_two, grad_value_two = lax.map(
        cross_backward,
        (split_heads(query_two), key_two, value_two, split_heads(grad_mixed_two), total_two),
    )
    flat_query_two = grad_query_two.reshape(group_rows, head_width)
    flat_key_two = grad_key_two.reshape(group_seqs * frames_all, head_width)
    flat_value_two = grad_value_two.reshape(group_seqs * frames_all, head_width)
    grad_cross_q = transposed(rows_two, flat_query_two) * head_scale
    bias_three = jnp.sum(flat_query_two.astype(jnp.float32), 0) * head_scale
    bias_four = jnp.sum(flat_value_two.astype(jnp.float32), 0)
    grad_cross_kv = jnp.stack(
        [transposed(flat_frames, flat_key_two), transposed(flat_frames, flat_value_two)]
    )
    grad_frames = against(flat_key_two, w_cross_kv[0]) + against(flat_value_two, w_cross_kv[1])
    grad_encoder = lax.psum_scatter(
        grad_frames.reshape(group_seqs, frames_all, width_all).astype(jnp.bfloat16),
        "tp",
        scatter_dimension=1,
        tiled=True,
    ).astype(jnp.float32)
    grad_normed_two = scatter_grads(against(flat_query_two, w_cross_q) * head_scale)
    gain_two = row_sum(grad_normed_two * unit_two)
    shift_two = row_sum(grad_normed_two)
    grad_first = grad_second + norm_back(grad_normed_two, unit_two, inv_two, gains[1])
    branch_one = grad_first.astype(jnp.bfloat16)
    bias_two = row_sum(branch_one.astype(jnp.float32))
    down_one = gather_grads(branch_one)
    grad_mixed_one = against(down_one, w_self_out).astype(jnp.bfloat16)
    grad_self_out = transposed(mixed_one, down_one)

    def self_backward(item):
        return attend_backward(item[0], item[1], item[2], item[3], item[4], self_mask(item[5]))

    grad_query_one, grad_key_one, grad_value_one = lax.map(
        self_backward,
        (
            split_heads(query_one),
            split_heads(key_one),
            split_heads(value_one),
            split_heads(grad_mixed_one),
            total_one,
            lengths,
        ),
    )
    flat_query_one = grad_query_one.reshape(group_rows, head_width)
    flat_key_one = grad_key_one.reshape(group_rows, head_width)
    flat_value_one = grad_value_one.reshape(group_rows, head_width)
    grad_qkv = jnp.stack(
        [
            transposed(rows_one, flat_query_one) * head_scale,
            transposed(rows_one, flat_key_one),
            transposed(rows_one, flat_value_one),
        ]
    )
    bias_zero = jnp.sum(flat_query_one.astype(jnp.float32), 0) * head_scale
    bias_one = jnp.sum(flat_value_one.astype(jnp.float32), 0)
    grad_normed_one = scatter_grads(
        against(flat_query_one, w_qkv[0]) * head_scale
        + against(flat_key_one, w_qkv[1])
        + against(flat_value_one, w_qkv[2])
    )
    gain_one = row_sum(grad_normed_one * unit_one)
    shift_one = row_sum(grad_normed_one)
    grad_inputs = grad_first + norm_back(grad_normed_one, unit_one, inv_one, gains[0])
    grad_gains = jnp.stack([gain_one, gain_two, gain_three, gain_four])
    grad_shifts = jnp.stack([shift_one, shift_two, shift_three, shift_four])
    grad_biases = jnp.stack(
        [
            placed(bias_zero),
            placed(bias_one),
            bias_two,
            placed(bias_three),
            placed(bias_four),
            bias_five,
            bias_six,
        ]
    )
    grad_fc_bias_all = lax.dynamic_update_slice_in_dim(
        jnp.zeros((ff_width * tp_count,), jnp.float32), grad_fc_bias, ff_start, 0
    )
    small_gain, small_shift, small_bias, small_fc_bias = (
        lax.psum_scatter(grad_gains, ("fsdp", "tp"), scatter_dimension=1, tiled=True),
        lax.psum_scatter(grad_shifts, ("fsdp", "tp"), scatter_dimension=1, tiled=True),
        lax.psum_scatter(grad_biases, ("fsdp", "tp"), scatter_dimension=1, tiled=True),
        lax.psum_scatter(grad_fc_bias_all, ("fsdp", "tp"), scatter_dimension=0, tiled=True),
    )
    (
        owned_qkv,
        owned_self_out,
        owned_cross_q,
        owned_cross_kv,
        owned_cross_out,
        owned_fc_in,
        owned_fc_out,
    ) = (
        lax.psum_scatter(grad_qkv, "fsdp", scatter_dimension=1, tiled=True),
        lax.psum_scatter(grad_self_out, "fsdp", scatter_dimension=1, tiled=True),
        lax.psum_scatter(grad_cross_q, "fsdp", scatter_dimension=0, tiled=True),
        lax.psum_scatter(grad_cross_kv, "fsdp", scatter_dimension=1, tiled=True),
        lax.psum_scatter(grad_cross_out, "fsdp", scatter_dimension=1, tiled=True),
        lax.psum_scatter(grad_fc_in, "fsdp", scatter_dimension=0, tiled=True),
        lax.psum_scatter(grad_fc_out, "fsdp", scatter_dimension=1, tiled=True),
    )
    return (
        result.astype(jnp.bfloat16),
        grad_inputs,
        grad_encoder,
        owned_qkv,
        owned_self_out,
        owned_cross_q,
        owned_cross_kv,
        owned_cross_out,
        owned_fc_in,
        owned_fc_out,
        small_gain,
        small_shift,
        small_bias,
        small_fc_bias,
    )


def solution(mesh):
    return jax.shard_map(
        local,
        mesh=mesh,
        in_specs=(
            P(("fsdp", "tp"), None, None),
            P("fsdp", "tp", None),
            P("fsdp"),
            P(None, "fsdp", "tp"),
            P("tp", "fsdp"),
            P("fsdp", "tp"),
            P(None, "fsdp", "tp"),
            P("tp", "fsdp"),
            P("fsdp", "tp"),
            P("tp", "fsdp"),
            P(None, ("fsdp", "tp")),
            P(None, ("fsdp", "tp")),
            P(None, ("fsdp", "tp")),
            P(("fsdp", "tp")),
            P(("fsdp", "tp"), None, None),
        ),
        out_specs=(
            P(("fsdp", "tp"), None, None),
            P(("fsdp", "tp"), None, None),
            P("fsdp", "tp", None),
            P(None, "fsdp", "tp"),
            P("tp", "fsdp"),
            P("fsdp", "tp"),
            P(None, "fsdp", "tp"),
            P("tp", "fsdp"),
            P("fsdp", "tp"),
            P("tp", "fsdp"),
            P(None, ("fsdp", "tp")),
            P(None, ("fsdp", "tp")),
            P(None, ("fsdp", "tp")),
            P(("fsdp", "tp")),
        ),
        check_vma=False,
    )
```

profile of v0, /device:TPU:0, one launch (start us, length us, event | category | flops | bytes accessed | tf_op | source)
XLA Modules:
  0.0 1686.6 jit_solution(319161292977433544)
XLA Ops:
  10.9 70.4 %all-gather = f32[32,24,4]{1,2,0:T(4,128)S(1)} all-gather(f32[1,24,4]{1,2,0:T(4,128)} %bitcast.408), channel_id=1, replica_groups=mesh['fsdp'=8,'tp'=4] {'fsdp','tp'}, dimensions={0}, use_global_device_ids=true | all-gather | bytes 12672 | tf_op jit(solution)/shard_map/all_gather | solution.py:122
  82.0 64.1 %all-gather.1 = f32[32,24,4]{1,2,0:T(4,128)S(1)} all-gather(f32[1,24,4]{1,2,0:T(4,128)} %bitcast.409), channel_id=1, replica_groups=mesh['fsdp'=8,'tp'=4] {'fsdp','tp'}, dimensions={0}, use_global_device_ids=true | all-gather | bytes 12672 | tf_op jit(solution)/shard_map/all_gather | solution.py:123
  149.3 69.4 %all-gather.2 = f32[32,24,7]{1,2,0:T(8,128)S(1)} all-gather(f32[1,24,7]{1,2,0:T(8,128)S(1)} %bitcast.407), channel_id=1, replica_groups=mesh['fsdp'=8,'tp'=4] {'fsdp','tp'}, dimensions={0}, use_global_device_ids=true | all-gather | bytes 22176 | tf_op jit(solution)/shard_map/all_gather | solution.py:124
  218.9 9.0 all_gather.59
  229.2 11.9 all_gather.57
  241.1 4.2 convolution_convert_fusion.9
  254.8 19.2 %while.58 = (s32[]{:T(128)}, bf16[4,448,3,64]{1,3,2,0:T(8,128)(2,1)S(1)}, f32[4,3,448,1]{2,1,3,0:T(4,128)}, bf16[4,448,3,64]{1,3,2,0:T(8,128)(2,1)S(1)}, s32[4]{...) while((s32[]{:T(128)}, ...), condition=%wide.region_5.6_spmd.clone.clone, body=%wide.region_2.5_spmd.clone.clone.sunk | while | flops 159960192 | bytes 9467121 | solution.py:182
  277.5 51.6 %reduce-scatter.27.cloned.1.call-done = bf16[1,448,768]{2,1,0:T(8,128)(2,1)} async-done(((bf16[4,448,768]{2,1,0:T(8,128)(2,1)}), bf16[1,448,768]{2,1,0:T(8,128)(2,1)}) %reduce-scatter.27.cloned.1.call-update) | async-done | bytes 688144 | tf_op jit(solution)/shard_map/reduce_scatter | solution.py:145
  334.3 9.5 all_gather.64
  343.8 9.7 all_gather.63
  355.0 10.8 all_gather.61
  365.8 24.4 %all-gather.17.cloned.1.call-done = bf16[4,448,768]{2,1,0:T(8,128)(2,1)} async-done(((bf16[1,448,768]{2,1,0:T(8,128)(2,1)}), bf16[4,448,768]{2,1,0:T(8,128)(2,1)}) %all-gather.17.cloned.1.call-update) | async-done | bytes 2752528 | tf_op jit(solution)/shard_map/all_gather | solution.py:141
  395.0 158.6 %all-gather.15.cloned.1.call-done = bf16[4,1500,768]{2,0,1:T(4,128)(2,1)} async-done(((bf16[4,375,768]{2,0,1:T(4,128)(2,1)}), bf16[4,1500,768]{2,0,1:T(4,128)(2,1)}) %all-gather.15.cloned.1.call-update) | async-done | bytes 9216016 | tf_op jit(solution)/shard_map/all_gather | solution.py:194
  553.6 8.4 copy.99
  561.9 10.7 reshape.514
  572.6 6.7 convolution_convert_fusion.4
  579.3 4.4 fusion.106
  583.8 5.8 reshape.515
  589.5 3.6 copy.100
  593.1 4.4 reshape.518
  600.6 29.4 %while.56 = (s32[]{:T(128)}, bf16[4,448,3,64]{1,3,2,0:T(8,128)(2,1)}, f32[4,3,448,1]{2,1,3,0:T(4,128)S(1)}, bf16[4,1500,3,64]{1,3,2,0:T(8,128)(2,1)}, bf16[4,448...) while((s32[]{:T(128)}, bf16[4,448,3,64]{1,3,2,0:T(8,128)(2,1)}, ...), condition=%wide.region_12.13_spmd, body=%wide.region_9.12_spmd.sunk | while | flops 528190656 | bytes 31719312 | solution.py:206
  629.9 3.6 convolution_convert_fusion.10
  634.2 52.0 %reduce-scatter.29.cloned.1.call-done = bf16[1,448,768]{2,1,0:T(8,128)(2,1)} async-done(((bf16[4,448,768]{2,1,0:T(8,128)(2,1)}), bf16[1,448,768]{2,1,0:T(8,128)(2,1)}) %reduce-scatter.29.cloned.1.call-update) | async-done | bytes 688144 | tf_op jit(solution)/shard_map/reduce_scatter | solution.py:145
  691.2 43.9 %all-reduce = f32[3072]{0:T(1024)S(1)} all-reduce(f32[3072]{0:T(1024)S(1)} %dynamic-update-slice), channel_id=1, replica_groups=mesh['fsdp'=8,'tp'=4] {'fsdp','tp'}, use_global_device_ids=true, to_apply=%add | all-reduce | flops 3072 | bytes 24576
  735.1 12.6 all-gather.19.cloned.1.call-done
  747.7 17.3 %multiply_convert_fusion.3 = (bf16[1792,768]{1,0:T(8,128)(2,1)}, f32[1792,768]{1,0:T(8,128)}, f32[1792,768]{1,0:T(8,128)}) fusion(f32[768]{0:T(1024)S(1)} %dynamic_slice.77, bf16[1792,768]{1,0:T(8,128)(2,1)} %bitcast.416, bf16[768,768]{1,0:T(8,128)(2,1)} %all-gather.21.cloned.1.call-done), kind=kOutput, calls=%fused_computation.124 | convolution fusion | flops 2204762112 | bytes 17697792 | tf_op jit(solution)/shard_map/dot_general | solution.py:28
  765.0 7.0 all-gather.23.cloned.1.call-done
  772.1 6.0 convolution_convert_fusion.6
  778.1 54.3 %reduce-scatter.31.cloned.1.call-done = bf16[1,448,768]{2,1,0:T(8,128)(2,1)} async-done(((bf16[4,448,768]{2,1,0:T(8,128)(2,1)}), bf16[1,448,768]{2,1,0:T(8,128)(2,1)}) %reduce-scatter.31.cloned.1.call-update) | async-done | bytes 688144 | tf_op jit(solution)/shard_map/reduce_scatter | solution.py:145
  838.0 56.2 %all-gather.25.cloned.1.call-done = bf16[4,448,768]{2,1,0:T(8,128)(2,1)} async-done(((bf16[1,448,768]{2,1,0:T(8,128)(2,1)}), bf16[4,448,768]{2,1,0:T(8,128)(2,1)}) %all-gather.25.cloned.1.call-update) | async-done | bytes 2752528 | tf_op jit(solution)/shard_map/all_gather | solution.py:153
  894.2 10.0 convert_reduce_fusion
  904.3 3.9 convolution_convert_fusion.5
  908.3 53.0 %reduce-scatter.33.cloned.1.call-done = bf16[1,448,768]{2,1,0:T(8,128)(2,1)} async-done(((bf16[4,448,768]{2,1,0:T(8,128)(2,1)}), bf16[1,448,768]{2,1,0:T(8,128)(2,1)}) %reduce-scatter.33.cloned.1.call-update) | async-done | bytes 688144 | tf_op jit(solution)/shard_map/reduce_scatter | solution.py:157
  964.3 4.1 convert_reduce_fusion.11
  968.7 56.2 %all-gather.27.cloned.1.call-done = bf16[4,448,768]{2,1,0:T(8,128)(2,1)} async-done(((bf16[1,448,768]{2,1,0:T(8,128)(2,1)}), bf16[4,448,768]{2,1,0:T(8,128)(2,1)}) %all-gather.27.cloned.1.call-update) | async-done | bytes 2752528 | tf_op jit(solution)/shard_map/all_gather | solution.py:153
  1024.9 3.7 convolution_convert_fusion.8
  1028.6 3.4 reshape.522
  1035.1 48.7 %while.57 = (s32[]{:T(128)}, bf16[4,448,3,64]{1,3,2,0:T(8,128)(2,1)}, bf16[4,1500,3,64]{1,3,2,0:T(8,128)(2,1)}, bf16[4,1500,3,64]{1,3,2,0:T(8,128)(2,1)}, bf16[4...) while((s32[]{:T(128)}, ...), condition=%wide.region_26.27_spmd, body=%wide.region_24.26_spmd.sunk | while | flops 1309044736 | bytes 67793800 | solution.py:240
  1038.7 3.1 multiply_reduce_fusion.7
  1063.1 3.1 multiply_reduce_fusion.7
  1075.2 3.1 multiply_reduce_fusion.7
  1090.1 52.8 %reduce-scatter.35.cloned.1.call-done = bf16[1,448,768]{2,1,0:T(8,128)(2,1)} async-done(((bf16[4,448,768]{2,1,0:T(8,128)(2,1)}), bf16[1,448,768]{2,1,0:T(8,128)(2,1)}) %reduce-scatter.35.cloned.1.call-update) | async-done | bytes 688144 | tf_op jit(solution)/shard_map/reduce_scatter | solution.py:157
  1159.2 3.2 copy.118
  1162.4 4.1 reshape.530
  1166.6 4.9 convolution_bitcast_fusion
  1172.1 6.6 convolution_bitcast_fusion.4
  1178.7 3.2 copy.117
  1181.9 4.1 reshape.529
  1186.1 5.7 convolution_bitcast_fusion.5
  1192.9 3.5 copy.141
  1196.4 3.2 reshape.549
  1199.9 10.1 fusion.163
  1210.0 13.0 add_convert_fusion
  1223.0 10.6 convert_element_type.240
  1233.6 36.9 %copy.119 = bf16[4,1500,768]{2,0,1:T(4,128)(2,1)} copy(bf16[4,1500,768]{2,1,0:T(8,128)(2,1)} %convert_element_type.240) | data formatting | bytes 18432000 | tf_op jit(solution)/shard_map/convert_element_type | solution.py:255
  1280.4 35.1 %while.59 = (s32[]{:T(128)}, bf16[4,448,3,64]{1,3,2,0:T(8,128)(2,1)}, bf16[4,448,3,64]{1,3,2,0:T(8,128)(2,1)}, bf16[4,448,3,64]{1,3,2,0:T(8,128)(2,1)}, bf16[4,4...) while((s32[]{:T(128)}, ...), condition=%wide.region_32.33_spmd.clone.clone, body=%wide.region_30.32_spmd.clone.clone.sunk | while | flops 390827136 | bytes 21527560 | solution.py:273
  1318.1 4.2 convolution_bitcast_fusion.1
  1322.8 3.3 convolution_bitcast_fusion.2
  1338.0 4.7 reshape.543
  1347.5 6.7 fusion.173
  1354.5 6.6 fusion.174
  1372.7 249.1 %all-reduce.9.cloned.1.call-done = bf16[4,1500,768]{2,0,1:T(4,128)(2,1)} async-done(((bf16[4,1500,768]{2,0,1:T(4,128)(2,1)}), bf16[4,1500,768]{2,0,1:T(4,128)(2,1)}) %all-reduce.9.cloned.1.call-update) | async-done | bytes 9216016
  1621.7 4.4 dynamic-slice_convert_fusion
  1632.6 40.6 %all-reduce.6 = (f32[4,768]{1,0:T(4,128)S(1)}, f32[4,768]{1,0:T(4,128)S(1)}, f32[7,768]{1,0:T(8,128)S(1)}, f32[3072]{0:T(1024)S(1)}) all-reduce(f32[4,768]{1,0:T(4,128)S(1)} %pad_maximum_fusion.2, f32[4,768]{1,0:T(4,128)S(1)} %pad_maximum_fusion.3, f32[7,768]{1,0:T(8,128)S(1)} %stack.96, ...), channel_id=16, replica_groups=mesh['fsdp'=8,'tp'=4] {'fsdp','tp'}, use_global_device_ids=true, to_apply=%region_48.49.clone | all-reduce | flops 14592 | bytes 116736
  (498 shorter events, 251.9 us)
Async XLA Ops:
  8.0 141.2 %copy-start.61 = (bf16[192,96]{1,0:T(8,128)(2,1)S(1)}, bf16[192,96]{1,0:T(8,128)(2,1)}, u32[]{:S(2)}) copy-start(bf16[192,96]{1,0:T(8,128)(2,1)} %param.27) | copy-start | bytes 110596
  8.0 141.3 %copy-start.77 = (f32[7,24]{1,0:T(8,128)S(1)}, f32[7,24]{1,0:T(8,128)}, u32[]{:S(2)}) copy-start(f32[7,24]{1,0:T(8,128)} %param.35) | copy-start | bytes 2020
  8.0 221.2 %copy-start.49 = (bf16[3,96,192]{2,1,0:T(8,128)(2,1)S(1)}, bf16[3,96,192]{2,1,0:T(8,128)(2,1)}, u32[]{:S(2)}) copy-start(bf16[3,96,192]{2,1,0:T(8,128)(2,1)} %param.26) | copy-start | bytes 331780
  8.0 233.0 %all-gather.13.cloned.1.call-start = ((), (), s32[]{:S(2)}) async-start(), calls=%async_computation.13 | async-start | bytes 3440640 | tf_op jit(solution)/shard_map/all_gather | solution.py:141
  9.4 139.9 %copy-start.56 = (f32[448]{0:T(512)}, f32[448]{0:T(512)S(1)}, u32[]{:S(2)}) copy-start(f32[448]{0:T(512)S(1)} %broadcast_multiply_fusion.13) | copy-start | bytes 5380
  10.9 138.4 %copy-start.63 = (f32[448]{0:T(512)}, f32[448]{0:T(512)S(1)}, u32[]{:S(2)}) copy-start(f32[448]{0:T(512)S(1)} %add_rsqrt_fusion.3) | copy-start | bytes 5380
  82.0 67.3 %copy-start.51 = (f32[768]{0:T(1024)}, f32[768]{0:T(1024)S(1)}, u32[]{:S(2)}) copy-start(f32[768]{0:T(1024)S(1)} %get-tuple-element.458) | copy-start | bytes 9220
  82.0 250.2 %copy-start.53 = (f32[768]{0:T(1024)}, f32[768]{0:T(1024)S(1)}, u32[]{:S(2)}) copy-start(f32[768]{0:T(1024)S(1)} %get-tuple-element.457) | copy-start | bytes 9220
  149.1 180.1 %reduce-scatter.27.cloned.1.call-start = ((), (), s32[]{:S(2)}) async-start(), calls=%async_computation.14 | async-start | bytes 3440640 | tf_op jit(solution)/shard_map/reduce_scatter | solution.py:145
  227.9 47.0 %copy-start.33 = (bf16[192,768]{0,1:T(8,128)(2,1)}, bf16[192,768]{0,1:T(8,128)(2,1)S(1)}, u32[]{:S(2)}) copy-start(bf16[192,768]{0,1:T(8,128)(2,1)S(1)} %all_gather.59) | copy-start | bytes 884740
  229.1 457.1 %copy-start.47 = (f32[768]{0:T(1024)}, f32[768]{0:T(1024)S(1)}, u32[]{:S(2)}) copy-start(f32[768]{0:T(1024)S(1)} %get-tuple-element.558) | copy-start | bytes 9220
  274.9 54.3 %copy-start = (bf16[1,448,768]{2,1,0:T(8,128)(2,1)S(1)}, bf16[1,448,768]{2,1,0:T(8,128)(2,1)}, u32[]{:S(2)}) copy-start(bf16[1,448,768]{2,1,0:T(8,128)(2,1)} %param.23) | copy-start | bytes 2064388
  277.4 54.8 %copy-start.69 = (f32[768]{0:T(1024)S(1)}, f32[768]{0:T(1024)}, u32[]{:S(2)}) copy-start(f32[768]{0:T(1024)} %get-tuple-element.461) | copy-start | bytes 9220
  277.5 112.8 %all-gather.17.cloned.1.call-start = ((), (), s32[]{:S(2)}) async-start(), calls=%async_computation.16 | async-start | bytes 3440640 | tf_op jit(solution)/shard_map/all_gather | solution.py:141
  332.2 11.6 copy-start.60
  332.2 22.8 %copy-start.50 = (bf16[2,96,192]{2,1,0:T(8,128)(2,1)S(1)}, bf16[2,96,192]{2,1,0:T(8,128)(2,1)}, u32[]{:S(2)}) copy-start(bf16[2,96,192]{2,1,0:T(8,128)(2,1)} %param.29) | copy-start | bytes 221188
  333.5 220.0 %all-gather.15.cloned.1.call-start = ((), (), s32[]{:S(2)}) async-start(), calls=%async_computation.15 | async-start | bytes 11520000 | tf_op jit(solution)/shard_map/all_gather | solution.py:194
  334.1 352.1 %reduce-scatter.29.cloned.1.call-start = ((), (), s32[]{:S(2)}) async-start(), calls=%async_computation.17 | async-start | bytes 3440640 | tf_op jit(solution)/shard_map/reduce_scatter | solution.py:145
  353.5 36.7 %copy-start.45 = (bf16[768,192]{1,0:T(8,128)(2,1)}, bf16[768,192]{1,0:T(8,128)(2,1)S(1)}, u32[]{:S(2)}) copy-start(bf16[768,192]{1,0:T(8,128)(2,1)S(1)} %all_gather.63) | copy-start | bytes 884740
  629.9 56.3 %copy-start.68 = (f32[768]{0:T(1024)S(1)}, f32[768]{0:T(1024)}, u32[]{:S(2)}) copy-start(f32[768]{0:T(1024)} %get-tuple-element.559) | copy-start | bytes 9220
  633.6 101.5 %all-gather.21.cloned.1.call-start = ((), (), s32[]{:S(2)}) async-start(), calls=%async_computation.19 | async-start | bytes 1327104 | tf_op jit(solution)/shard_map/all_gather | solution.py:118
  634.2 113.5 %all-gather.19.cloned.1.call-start = ((), (), s32[]{:S(2)}) async-start(), calls=%async_computation.18 | async-start | bytes 3440640 | tf_op jit(solution)/shard_map/all_gather | solution.py:141
  690.2 81.8 %all-gather.23.cloned.1.call-start = ((), (), s32[]{:S(2)}) async-start(), calls=%async_computation.20 | async-start | bytes 1327104 | tf_op jit(solution)/shard_map/all_gather | solution.py:119
  690.8 141.7 %reduce-scatter.31.cloned.1.call-start = ((), (), s32[]{:S(2)}) async-start(), calls=%async_computation.21 | async-start | bytes 3440640 | tf_op jit(solution)/shard_map/reduce_scatter | solution.py:145
  778.0 54.4 %copy-start.67 = (f32[768]{0:T(1024)S(1)}, f32[768]{0:T(1024)}, u32[]{:S(2)}) copy-start(f32[768]{0:T(1024)} %get-tuple-element.560) | copy-start | bytes 9220
  778.1 56.5 %copy-start.26 = (bf16[1,448,768]{2,1,0:T(8,128)(2,1)S(1)}, bf16[1,448,768]{2,1,0:T(8,128)(2,1)}, u32[]{:S(2)}) copy-start(bf16[1,448,768]{2,1,0:T(8,128)(2,1)} %param.37) | copy-start | bytes 2064388
  778.1 56.5 %copy-start.55 = (f32[768]{0:T(1024)S(1)}, f32[768]{0:T(1024)}, u32[]{:S(2)}) copy-start(f32[768]{0:T(1024)} %get-tuple-element.455) | copy-start | bytes 9220
  778.1 116.2 %all-gather.25.cloned.1.call-start = ((), (), s32[]{:S(2)}) async-start(), calls=%async_computation.22 | async-start | bytes 3440640 | tf_op jit(solution)/shard_map/all_gather | solution.py:153
  837.8 123.6 %reduce-scatter.33.cloned.1.call-start = ((), (), s32[]{:S(2)}) async-start(), calls=%async_computation.23 | async-start | bytes 3440640 | tf_op jit(solution)/shard_map/reduce_scatter | solution.py:157
  894.2 10.0 copy-start.79
  908.2 56.1 %copy-start.75 = (f32[768]{0:T(1024)S(1)}, f32[768]{0:T(1024)}, u32[]{:S(2)}) copy-start(f32[768]{0:T(1024)} %get-tuple-element.459) | copy-start | bytes 9220
  908.2 116.6 %all-gather.27.cloned.1.call-start = ((), (), s32[]{:S(2)}) async-start(), calls=%async_computation.24 | async-start | bytes 3440640 | tf_op jit(solution)/shard_map/all_gather | solution.py:153
  968.4 174.5 %reduce-scatter.35.cloned.1.call-start = ((), (), s32[]{:S(2)}) async-start(), calls=%async_computation.25 | async-start | bytes 3440640 | tf_op jit(solution)/shard_map/reduce_scatter | solution.py:157
  1087.2 55.7 %copy-start.1 = (bf16[1,448,768]{2,1,0:T(8,128)(2,1)S(1)}, bf16[1,448,768]{2,1,0:T(8,128)(2,1)}, u32[]{:S(2)}) copy-start(bf16[1,448,768]{2,1,0:T(8,128)(2,1)} %param.23) | copy-start | bytes 2064388
  1087.2 55.7 %copy-start.7 = (bf16[1,448,768]{2,1,0:T(8,128)(2,1)S(1)}, bf16[1,448,768]{2,1,0:T(8,128)(2,1)}, u32[]{:S(2)}) copy-start(bf16[1,448,768]{2,1,0:T(8,128)(2,1)} %reduce-scatter.27.cloned.1.call-done) | copy-start | bytes 2064388
  1087.2 55.7 %copy-start.48 = (f32[768]{0:T(1024)S(1)}, f32[768]{0:T(1024)}, u32[]{:S(2)}) copy-start(f32[768]{0:T(1024)} %copy-done.47) | copy-start | bytes 9220
  1087.2 55.7 %copy-start.54 = (f32[768]{0:T(1024)S(1)}, f32[768]{0:T(1024)}, u32[]{:S(2)}) copy-start(f32[768]{0:T(1024)} %copy-done.53) | copy-start | bytes 9220
  1087.2 55.7 %copy-start.59 = (f32[448]{0:T(512)S(1)}, f32[448]{0:T(512)}, u32[]{:S(2)}) copy-start(f32[448]{0:T(512)} %copy-done.58) | copy-start | bytes 5380
  1087.2 55.7 %copy-start.66 = (f32[448]{0:T(512)S(1)}, f32[448]{0:T(512)}, u32[]{:S(2)}) copy-start(f32[448]{0:T(512)} %copy-done.65) | copy-start | bytes 5380
  1089.7 55.1 %copy-start.27 = (f32[1,448,768]{2,1,0:T(8,128)S(1)}, f32[1,448,768]{2,1,0:T(8,128)}, u32[]{:S(2)}) copy-start(f32[1,448,768]{2,1,0:T(8,128)} %get-tuple-element.537) | copy-start | bytes 4128772
  1089.8 181.1 %all-gather.29.cloned.1.call-start = ((), (), s32[]{:S(2)}) async-start(), calls=%async_computation.26 | async-start | bytes 3440640 | tf_op jit(solution)/shard_map/all_gather | solution.py:153
  1148.0 221.2 %reduce-scatter.51.cloned.1.call-start = ((), (), s32[]{:S(2)}) async-start(), calls=%async_computation.34 | async-start | bytes 884736
  1148.1 11.1 copy-start.14
  1171.5 199.3 %reduce-scatter.49.cloned.1.call-start = ((), (), s32[]{:S(2)}) async-start(), calls=%async_computation.33 | async-start | bytes 1327104
  1199.7 422.1 %all-reduce.9.cloned.1.call-start = ((), (), s32[]{:S(2)}) async-start(), calls=%async_computation.35 | async-start | bytes 18432000
  1199.9 10.2 copy-start.17
  1199.9 10.1 copy-start.31
  1270.6 356.5 %reduce-scatter.45.cloned.1.call-start = ((), (), s32[]{:S(2)}) async-start(), calls=%async_computation.31 | async-start | bytes 884736
  1322.3 7.4 copy-start.19
  1322.3 306.5 %reduce-scatter.43.cloned.1.call-start = ((), (), s32[]{:S(2)}) async-start(), calls=%async_computation.30 | async-start | bytes 2211840
  1342.7 287.9 %reduce-scatter.37.cloned.1.call-start = ((), (), s32[]{:S(2)}) async-start(), calls=%async_computation.27 | async-start | bytes 3440640 | tf_op jit(solution)/shard_map/reduce_scatter | solution.py:157
  1347.5 331.4 %reduce-scatter.39.cloned.1.call-start = ((), (), s32[]{:S(2)}) async-start(), calls=%async_computation.28 | async-start | bytes 2654208 | tf_op jit(solution)/shard_map/reduce_scatter | solution.py:340
  1354.2 7.0 copy-start.82
  1354.2 8.3 copy-start.71
  1354.2 8.3 copy-start.70
  1354.3 8.3 copy-start.72
  1354.3 8.3 copy-start.78
  1354.3 8.6 copy-start.74
  1354.3 8.6 copy-start.76
  1354.3 8.7 copy-start.73
  1354.3 324.5 %reduce-scatter.41.cloned.1.call-start = ((), (), s32[]{:S(2)}) async-start(), calls=%async_computation.29 | async-start | bytes 2654208 | tf_op jit(solution)/shard_map/reduce_scatter | solution.py:341
  1361.2 317.7 %reduce-scatter.47.cloned.1.call-start = ((), (), s32[]{:S(2)}) async-start(), calls=%async_computation.32 | async-start | bytes 884736
  1372.6 253.5 %copy-start.18 = (bf16[4,448,3,64]{1,3,2,0:T(8,128)(2,1)S(1)}, bf16[4,448,3,64]{1,3,2,0:T(8,128)(2,1)}, u32[]{:S(2)}) copy-start(bf16[4,448,3,64]{1,3,2,0:T(8,128)(2,1)} %get-tuple-element.211) | copy-start | bytes 2064388
  1372.7 253.7 %copy-start.20 = (bf16[4,448,3,64]{1,3,2,0:T(8,128)(2,1)S(1)}, bf16[4,448,3,64]{1,3,2,0:T(8,128)(2,1)}, u32[]{:S(2)}) copy-start(bf16[4,448,3,64]{1,3,2,0:T(8,128)(2,1)} %get-tuple-element.209) | copy-start | bytes 2064388
  (52 other events, 161.8 us)
Sparse Core Ops, SparseCore 0:
  149.2 56.4 all-gather.12
  277.6 51.5 reduce-scatter.26
  333.7 56.5 all-gather.16
  391.7 161.8 all-gather.14
  633.7 52.4 reduce-scatter.28
  1270.7 351.0 all-reduce.8
Sparse Core Ops, SparseCore 1:
  636.0 22.0 all-gather.20
  690.3 57.4 all-gather.18
  749.5 22.5 all-gather.22
  778.1 54.3 reduce-scatter.30
  837.9 56.3 all-gather.24
  908.3 53.0 reduce-scatter.32
  968.5 56.4 all-gather.26
  1089.9 53.0 reduce-scatter.34
  1148.1 56.4 all-gather.28
  1207.7 33.6 reduce-scatter.50
  1244.4 36.6 reduce-scatter.48
  1322.4 34.5 reduce-scatter.44
  1360.2 40.0 reduce-scatter.42
  1402.6 120.2 reduce-scatter.36
  1526.8 42.2 reduce-scatter.38
  1573.0 42.2 reduce-scatter.40
  1619.0 35.1 reduce-scatter.46
where the time goes:
time: 1690 us
  waiting for transfers between devices  830 us (49%)
  blocking collectives  339 us (20%)
  matrix products  238 us (14%)
  local copies, waits for them, and re-layouts  189 us (11%)
  other arithmetic  68.7 us (4%)
  between operations  18.1 us (1%)
    unnamed x29, waiting for transfers between devices  251 us
    all_gather x1, waiting for transfers between devices, local(): frames = lax.all_gather(encoder, 'tp', axis=1, tiled=True)  159 us
    reduce_scatter x3, waiting for transfers between devices, scatter_rows(): lax.psum_scatter(partial_out.reshape(group_seqs, seq_len, width_all).asty...  158 us
    all_gather x3, waiting for transfers between devices, gather_grads(): whole = lax.all_gather(grad_rows, 'tp', axis=0, tiled=True)  112 us
    reduce_scatter x3, waiting for transfers between devices, scatter_grads(): lax.psum_scatter(partial_grad.reshape(group_seqs, seq_len, width_all).ast...  106 us
    unnamed x2, blocking collectives  84.5 us
    all_gather x1, blocking collectives, local(): lax.all_gather(norm_gain, ('fsdp', 'tp'), axis=1, tiled=True)  70.4 us
    all_gather x1, blocking collectives, local(): lax.all_gather(proj_bias, ('fsdp', 'tp'), axis=1, tiled=True)  69.4 us
  transfers between devices with their start and end apart: 23, of which 12 were waited for; matrix products, arithmetic and copies ran while one was open for 16% of the time, Pallas kernels for 0%

commit v1 on v0

--- a/solution.py
+++ b/solution.py
@@ -6,6 +6,19 @@
 HD = 64
 EPSILON = 1e-05
 NEGATIVE = -1e30
+
+
+def collect(x, axis, dim):
+    ways = lax.axis_size(axis)
+    up = [(d, (d + 1) % ways) for d in range(ways)]
+    down = [(d, (d - 1) % ways) for d in range(ways)]
+    earlier, later = ([x], [x])
+    for _ in range(ways // 2):
+        earlier.append(lax.ppermute(earlier[-1], axis, up))
+    for _ in range((ways - 1) // 2):
+        later.append(lax.ppermute(later[-1], axis, down))
+    line = jnp.concatenate([*earlier[::-1], *later[1:]], axis=dim)
+    return jnp.roll(line, (lax.axis_index(axis) - ways // 2) * x.shape[dim], axis=dim)
 
 
 def normalize(row_block, gain_row, shift_row):
@@ -191,7 +204,7 @@
         jnp.bfloat16
     )
     head_shape = (group_seqs, frames_all, local_heads, HD)
-    frames = lax.all_gather(encoder, "tp", axis=1, tiled=True)
+    frames = collect(encoder, "tp", 1)
     flat_frames = frames.reshape(group_seqs * frames_all, width_all)
     key_two = matmul(flat_frames, w_cross_kv[0]).astype(jnp.bfloat16).reshape(head_shape)
     value_two = (

time: 1690 us -> 1690 us (level)
  waiting for transfers between devices: 830 us -> 794 us
  local copies, waits for them, and re-layouts: 189 us -> 210 us
    ppermute x0 -> x3, waiting for transfers between devices: none -> 199 us  [the longest x2 150 us: collect(): earlier.append(lax.ppermute(earlier[-1], axis, up))]
    all_gather x1 -> x0, waiting for transfers between devices: 159 us -> none  [local(): frames = lax.all_gather(encoder, 'tp', axis=1, tiled=True)]
    reduce_scatter x3, waiting for transfers between devices: 158 us -> 107 us  [scatter_rows(): lax.psum_scatter(partial_out.reshape(group_seqs, seq_len, width_all).asty...]
    all_gather x3, waiting for transfers between devices: 37 us -> 12.7 us  [gather_rows(): lax.all_gather(normed.astype(jnp.bfloat16), 'tp', axis=0, tiled=True)]
    unnamed x190 -> x197, local copies, waits for them, and re-layouts: 32.3 us -> 44.5 us
    unnamed x29 -> x28, waiting for transfers between devices: 251 us -> 250 us
  transfers between devices with their start and end apart: 23 -> 25, of which waited for: 12 -> 12; matrix products, arithmetic and copies ran while one was open for 16% -> 20% of each run, Pallas kernels for 0% -> 0%
where the time goes in v1:
time: 1690 us; the launch traced here: 1680 us
  waiting for transfers between devices  794 us (47%)
  blocking collectives  340 us (20%)
  matrix products  243 us (14%)
  local copies, waits for them, and re-layouts  210 us (12%)
  other arithmetic  68.7 us (4%)
  between operations  18.2 us (1%)
    unnamed x28, waiting for transfers between devices  250 us
    ppermute x2, waiting for transfers between devices, collect(): earlier.append(lax.ppermute(earlier[-1], axis, up))  150 us
    all_gather x3, waiting for transfers between devices, gather_grads(): whole = lax.all_gather(grad_rows, 'tp', axis=0, tiled=True)  112 us
    reduce_scatter x3, waiting for transfers between devices, scatter_rows(): lax.psum_scatter(partial_out.reshape(group_seqs, seq_len, width_all).asty...  107 us
    reduce_scatter x3, waiting for transfers between devices, scatter_grads(): lax.psum_scatter(partial_grad.reshape(group_seqs, seq_len, width_all).ast...  106 us
    unnamed x2, blocking collectives  84.5 us
    all_gather x1, blocking collectives, local(): lax.all_gather(norm_gain, ('fsdp', 'tp'), axis=1, tiled=True)  70.4 us
    all_gather x1, blocking collectives, local(): lax.all_gather(proj_bias, ('fsdp', 'tp'), axis=1, tiled=True)  69.4 us
  transfers between devices with their start and end apart: 25, of which 12 were waited for; matrix products, arithmetic and copies ran while one was open for 20% of the time, Pallas kernels for 0%

profile of v1, /device:TPU:0, one launch (start us, length us, event | category | flops | bytes accessed | tf_op | source)
XLA Modules:
  0.0 1681.2 jit_solution(12278374822525854724)
XLA Ops:
  10.9 70.4 %all-gather = f32[32,24,4]{1,2,0:T(4,128)S(1)} all-gather(f32[1,24,4]{1,2,0:T(4,128)} %bitcast.404), channel_id=1, replica_groups=mesh['fsdp'=8,'tp'=4] {'fsdp','tp'}, dimensions={0}, use_global_device_ids=true | all-gather | bytes 12672 | tf_op jit(solution)/shard_map/all_gather | solution.py:135
  82.0 64.1 %all-gather.1 = f32[32,24,4]{1,2,0:T(4,128)S(1)} all-gather(f32[1,24,4]{1,2,0:T(4,128)} %bitcast.405), channel_id=1, replica_groups=mesh['fsdp'=8,'tp'=4] {'fsdp','tp'}, dimensions={0}, use_global_device_ids=true | all-gather | bytes 12672 | tf_op jit(solution)/shard_map/all_gather | solution.py:136
  149.3 69.4 %all-gather.2 = f32[32,24,7]{1,2,0:T(8,128)S(1)} all-gather(f32[1,24,7]{1,2,0:T(8,128)S(1)} %bitcast.403), channel_id=1, replica_groups=mesh['fsdp'=8,'tp'=4] {'fsdp','tp'}, dimensions={0}, use_global_device_ids=true | all-gather | bytes 22176 | tf_op jit(solution)/shard_map/all_gather | solution.py:137
  218.9 9.0 all_gather.56
  229.2 11.9 all_gather.54
  241.1 4.2 convolution_convert_fusion.9
  254.8 19.2 %while.58 = (s32[]{:T(128)}, bf16[4,448,3,64]{1,3,2,0:T(8,128)(2,1)S(1)}, f32[4,3,448,1]{2,1,3,0:T(4,128)}, bf16[4,448,3,64]{1,3,2,0:T(8,128)(2,1)S(1)}, s32[4]{...) while((s32[]{:T(128)}, ...), condition=%wide.region_5.6_spmd.clone.clone, body=%wide.region_2.5_spmd.clone.clone.sunk | while | flops 159960192 | bytes 9467121 | solution.py:195
  278.2 98.0 %collective-permute-done = bf16[4,375,768]{2,0,1:T(4,128)(2,1)S(1)} collective-permute-done((bf16[4,375,768]{2,0,1:T(4,128)(2,1)}, bf16[4,375,768]{2,0,1:T(4,128)(2,1)S(1)}, u32[]{:S(2)}, u32[]{:S(2)}) %collective-permute-start) | collective-permute-done | bytes 2304032 | tf_op jit(solution)/shard_map/ppermute | solution.py:17
  376.2 3.8 collective-permute-start.2
  384.6 9.2 all_gather.60
  393.8 10.4 all_gather.59
  405.0 10.9 all_gather.57
  416.0 51.8 %collective-permute-done.1 = bf16[4,375,768]{2,0,1:T(4,128)(2,1)} collective-permute-done((bf16[4,375,768]{2,0,1:T(4,128)(2,1)S(1)}, bf16[4,375,768]{2,0,1:T(4,128)(2,1)}, u32[]{:S(2)}, u32[]{:S(2)}) %collective-permute-start.1) | collective-permute-done | bytes 2304032 | tf_op jit(solution)/shard_map/ppermute | solution.py:17
  472.9 48.7 %collective-permute-done.2 = bf16[4,375,768]{2,0,1:T(4,128)(2,1)} collective-permute-done((bf16[4,375,768]{2,0,1:T(4,128)(2,1)}, bf16[4,375,768]{2,0,1:T(4,128)(2,1)}, u32[]{:S(2)}, u32[]{:S(2)}) %collective-permute-start.2) | collective-permute-done | bytes 2304032 | tf_op jit(solution)/shard_map/ppermute | solution.py:19
  531.6 5.3 constant_dynamic-slice_fusion.5
  536.9 8.4 copy.99
  545.2 10.8 reshape.514
  556.0 7.9 fusion.106
  563.9 4.8 reshape.515
  570.6 6.5 convolution_convert_fusion.4
  577.2 4.4 reshape.518
  583.8 3.7 fusion.117
  587.5 3.7 reshape.517
  594.5 29.1 %while.56 = (s32[]{:T(128)}, bf16[4,448,3,64]{1,3,2,0:T(8,128)(2,1)}, f32[4,3,448,1]{2,1,3,0:T(4,128)S(1)}, bf16[4,1500,3,64]{1,3,2,0:T(8,128)(2,1)}, bf16[4,448...) while((s32[]{:T(128)}, bf16[4,448,3,64]{1,3,2,0:T(8,128)(2,1)}, ...), condition=%wide.region_12.13_spmd, body=%wide.region_9.12_spmd.sunk | while | flops 528190656 | bytes 31719312 | solution.py:219
  623.6 3.6 convolution_convert_fusion.10
  627.9 52.6 %reduce-scatter.29.cloned.1.call-done = bf16[1,448,768]{2,1,0:T(8,128)(2,1)} async-done(((bf16[4,448,768]{2,1,0:T(8,128)(2,1)}), bf16[1,448,768]{2,1,0:T(8,128)(2,1)}) %reduce-scatter.29.cloned.1.call-update) | async-done | bytes 688144 | tf_op jit(solution)/shard_map/reduce_scatter | solution.py:158
  685.5 43.9 %all-reduce = f32[3072]{0:T(1024)S(1)} all-reduce(f32[3072]{0:T(1024)S(1)} %dynamic-update-slice), channel_id=1, replica_groups=mesh['fsdp'=8,'tp'=4] {'fsdp','tp'}, use_global_device_ids=true, to_apply=%add | all-reduce | flops 3072 | bytes 24576
  729.5 12.7 all-gather.16.cloned.1.call-done
  742.1 17.3 %multiply_convert_fusion.3 = (bf16[1792,768]{1,0:T(8,128)(2,1)}, f32[1792,768]{1,0:T(8,128)}, f32[1792,768]{1,0:T(8,128)}) fusion(f32[768]{0:T(1024)S(1)} %dynamic_slice.82, bf16[1792,768]{1,0:T(8,128)(2,1)} %bitcast.412, bf16[768,768]{1,0:T(8,128)(2,1)} %all-gather.18.cloned.1.call-done), kind=kOutput, calls=%fused_computation.124 | convolution fusion | flops 2204762112 | bytes 17697792 | tf_op jit(solution)/shard_map/dot_general | solution.py:41
  759.4 7.0 all-gather.20.cloned.1.call-done
  766.4 6.0 convolution_convert_fusion.6
  772.5 54.3 %reduce-scatter.31.cloned.1.call-done = bf16[1,448,768]{2,1,0:T(8,128)(2,1)} async-done(((bf16[4,448,768]{2,1,0:T(8,128)(2,1)}), bf16[1,448,768]{2,1,0:T(8,128)(2,1)}) %reduce-scatter.31.cloned.1.call-update) | async-done | bytes 688144 | tf_op jit(solution)/shard_map/reduce_scatter | solution.py:158
  832.4 56.2 %all-gather.22.cloned.1.call-done = bf16[4,448,768]{2,1,0:T(8,128)(2,1)} async-done(((bf16[1,448,768]{2,1,0:T(8,128)(2,1)}), bf16[4,448,768]{2,1,0:T(8,128)(2,1)}) %all-gather.22.cloned.1.call-update) | async-done | bytes 2752528 | tf_op jit(solution)/shard_map/all_gather | solution.py:166
  888.6 10.0 convert_reduce_fusion
  898.6 3.9 convolution_convert_fusion.5
  902.6 53.1 %reduce-scatter.33.cloned.1.call-done = bf16[1,448,768]{2,1,0:T(8,128)(2,1)} async-done(((bf16[4,448,768]{2,1,0:T(8,128)(2,1)}), bf16[1,448,768]{2,1,0:T(8,128)(2,1)}) %reduce-scatter.33.cloned.1.call-update) | async-done | bytes 688144 | tf_op jit(solution)/shard_map/reduce_scatter | solution.py:170
  958.7 4.1 convert_reduce_fusion.11
  963.2 56.2 %all-gather.24.cloned.1.call-done = bf16[4,448,768]{2,1,0:T(8,128)(2,1)} async-done(((bf16[1,448,768]{2,1,0:T(8,128)(2,1)}), bf16[4,448,768]{2,1,0:T(8,128)(2,1)}) %all-gather.24.cloned.1.call-update) | async-done | bytes 2752528 | tf_op jit(solution)/shard_map/all_gather | solution.py:166
  1019.4 3.7 convolution_convert_fusion.8
  1023.1 3.4 reshape.522
  1029.7 48.7 %while.57 = (s32[]{:T(128)}, bf16[4,448,3,64]{1,3,2,0:T(8,128)(2,1)}, bf16[4,1500,3,64]{1,3,2,0:T(8,128)(2,1)}, bf16[4,1500,3,64]{1,3,2,0:T(8,128)(2,1)}, bf16[4...) while((s32[]{:T(128)}, ...), condition=%wide.region_26.27_spmd, body=%wide.region_24.26_spmd.sunk | while | flops 1309044736 | bytes 67793800 | solution.py:253
  1084.6 53.0 %reduce-scatter.35.cloned.1.call-done = bf16[1,448,768]{2,1,0:T(8,128)(2,1)} async-done(((bf16[4,448,768]{2,1,0:T(8,128)(2,1)}), bf16[1,448,768]{2,1,0:T(8,128)(2,1)}) %reduce-scatter.35.cloned.1.call-update) | async-done | bytes 688144 | tf_op jit(solution)/shard_map/reduce_scatter | solution.py:170
  1153.8 3.2 copy.118
  1157.0 4.1 reshape.530
  1161.2 4.9 convolution_bitcast_fusion
  1166.4 6.6 convolution_bitcast_fusion.4
  1173.1 3.2 copy.117
  1176.3 4.1 reshape.529
  1180.5 5.7 convolution_bitcast_fusion.5
  1187.3 3.5 copy.141
  1190.8 3.2 reshape.549
  1194.4 10.1 fusion.163
  1204.5 13.0 add_convert_fusion
  1217.5 10.6 convert_element_type.240
  1228.1 36.9 %copy.119 = bf16[4,1500,768]{2,0,1:T(4,128)(2,1)} copy(bf16[4,1500,768]{2,1,0:T(8,128)(2,1)} %convert_element_type.240) | data formatting | bytes 18432000 | tf_op jit(solution)/shard_map/convert_element_type | solution.py:268
  1274.8 35.1 %while.59 = (s32[]{:T(128)}, bf16[4,448,3,64]{1,3,2,0:T(8,128)(2,1)}, bf16[4,448,3,64]{1,3,2,0:T(8,128)(2,1)}, bf16[4,448,3,64]{1,3,2,0:T(8,128)(2,1)}, bf16[4,4...) while((s32[]{:T(128)}, ...), condition=%wide.region_32.33_spmd.clone.clone, body=%wide.region_30.32_spmd.clone.clone.sunk | while | flops 390827136 | bytes 21527560 | solution.py:286
  1312.6 4.2 convolution_bitcast_fusion.1
  1317.0 3.4 convolution_bitcast_fusion.2
  1332.3 4.7 reshape.543
  1341.9 6.7 fusion.173
  1348.9 6.6 fusion.174
  1367.1 249.1 %all-reduce.9.cloned.1.call-done = bf16[4,1500,768]{2,0,1:T(4,128)(2,1)} async-done(((bf16[4,1500,768]{2,0,1:T(4,128)(2,1)}), bf16[4,1500,768]{2,0,1:T(4,128)(2,1)}) %all-reduce.9.cloned.1.call-update) | async-done | bytes 9216016
  1616.2 4.4 dynamic-slice_convert_fusion
  1627.0 40.7 %all-reduce.6 = (f32[4,768]{1,0:T(4,128)S(1)}, f32[4,768]{1,0:T(4,128)S(1)}, f32[7,768]{1,0:T(8,128)S(1)}, f32[3072]{0:T(1024)S(1)}) all-reduce(f32[4,768]{1,0:T(4,128)S(1)} %pad_maximum_fusion.2, f32[4,768]{1,0:T(4,128)S(1)} %pad_maximum_fusion.3, f32[7,768]{1,0:T(8,128)S(1)} %stack.96, ...), channel_id=16, replica_groups=mesh['fsdp'=8,'tp'=4] {'fsdp','tp'}, use_global_device_ids=true, to_apply=%region_48.49.clone | all-reduce | flops 14592 | bytes 116736
  (510 shorter events, 275.2 us)
Async XLA Ops:
  8.0 141.2 %copy-start.61 = (bf16[192,96]{1,0:T(8,128)(2,1)S(1)}, bf16[192,96]{1,0:T(8,128)(2,1)}, u32[]{:S(2)}) copy-start(bf16[192,96]{1,0:T(8,128)(2,1)} %param.27) | copy-start | bytes 110596
  8.0 141.3 %copy-start.77 = (f32[7,24]{1,0:T(8,128)S(1)}, f32[7,24]{1,0:T(8,128)}, u32[]{:S(2)}) copy-start(f32[7,24]{1,0:T(8,128)} %param.35) | copy-start | bytes 2020
  8.0 221.2 %copy-start.49 = (bf16[3,96,192]{2,1,0:T(8,128)(2,1)S(1)}, bf16[3,96,192]{2,1,0:T(8,128)(2,1)}, u32[]{:S(2)}) copy-start(bf16[3,96,192]{2,1,0:T(8,128)(2,1)} %param.26) | copy-start | bytes 331780
  8.0 233.0 %all-gather.12.cloned.1.call-start = ((), (), s32[]{:S(2)}) async-start(), calls=%async_computation.13 | async-start | bytes 3440640 | tf_op jit(solution)/shard_map/all_gather | solution.py:154
  9.4 139.9 %copy-start.57 = (f32[448]{0:T(512)}, f32[448]{0:T(512)S(1)}, u32[]{:S(2)}) copy-start(f32[448]{0:T(512)S(1)} %broadcast_multiply_fusion.13) | copy-start | bytes 5380
  10.9 138.4 %copy-start.63 = (f32[448]{0:T(512)}, f32[448]{0:T(512)S(1)}, u32[]{:S(2)}) copy-start(f32[448]{0:T(512)S(1)} %add_rsqrt_fusion.3) | copy-start | bytes 5380
  82.0 67.3 %copy-start.51 = (f32[768]{0:T(1024)}, f32[768]{0:T(1024)S(1)}, u32[]{:S(2)}) copy-start(f32[768]{0:T(1024)S(1)} %get-tuple-element.458) | copy-start | bytes 9220
  82.0 301.1 %copy-start.53 = (f32[768]{0:T(1024)}, f32[768]{0:T(1024)S(1)}, u32[]{:S(2)}) copy-start(f32[768]{0:T(1024)S(1)} %get-tuple-element.457) | copy-start | bytes 9220
  149.1 230.9 %reduce-scatter.27.cloned.1.call-start = ((), (), s32[]{:S(2)}) async-start(), calls=%async_computation.14 | async-start | bytes 3440640 | tf_op jit(solution)/shard_map/reduce_scatter | solution.py:158
  227.9 47.0 %copy-start.34 = (bf16[192,768]{0,1:T(8,128)(2,1)}, bf16[192,768]{0,1:T(8,128)(2,1)S(1)}, u32[]{:S(2)}) copy-start(bf16[192,768]{0,1:T(8,128)(2,1)S(1)} %all_gather.56) | copy-start | bytes 884740
  229.1 451.5 %copy-start.47 = (f32[768]{0:T(1024)}, f32[768]{0:T(1024)S(1)}, u32[]{:S(2)}) copy-start(f32[768]{0:T(1024)S(1)} %get-tuple-element.558) | copy-start | bytes 9220
  274.9 105.1 %copy-start = (bf16[1,448,768]{2,1,0:T(8,128)(2,1)S(1)}, bf16[1,448,768]{2,1,0:T(8,128)(2,1)}, u32[]{:S(2)}) copy-start(bf16[1,448,768]{2,1,0:T(8,128)(2,1)} %param.23) | copy-start | bytes 2064388
  277.5 306.3 %all-gather.14.cloned.1.call-start = ((), (), s32[]{:S(2)}) async-start(), calls=%async_computation.15 | async-start | bytes 3440640 | tf_op jit(solution)/shard_map/all_gather | solution.py:154
  277.5 98.7 %collective-permute-start = (bf16[4,375,768]{2,0,1:T(4,128)(2,1)}, bf16[4,375,768]{2,0,1:T(4,128)(2,1)S(1)}, u32[]{:S(2)}, u32[]{:S(2)}) collective-permute-start(bf16[4,375,768]{2,0,1:T(4,128)(2,1)} %param.24), channel_id=1, source_target_pairs={{0,1},{1,2},{2,3},{3,0},{4,5},{5,6},{6,7},{7,4},{8,9},{9,10},{10,1... | collective-permute-start | bytes 6912008 | tf_op jit(solution)/shard_map/ppermute | solution.py:17
  376.2 91.6 %collective-permute-start.1 = (bf16[4,375,768]{2,0,1:T(4,128)(2,1)S(1)}, bf16[4,375,768]{2,0,1:T(4,128)(2,1)}, u32[]{:S(2)}, u32[]{:S(2)}) collective-permute-start(bf16[4,375,768]{2,0,1:T(4,128)(2,1)S(1)} %collective-permute-done), channel_id=1, source_target_pairs={{0,1},{1,2},{2,3},{3,0},{4,5},{5,6},{6,7},{7,4},{8,9},{9,10},{10,1... | collective-permute-start | bytes 6912008 | tf_op jit(solution)/shard_map/ppermute | solution.py:17
  376.2 145.4 %collective-permute-start.2 = (bf16[4,375,768]{2,0,1:T(4,128)(2,1)}, bf16[4,375,768]{2,0,1:T(4,128)(2,1)}, u32[]{:S(2)}, u32[]{:S(2)}) collective-permute-start(bf16[4,375,768]{2,0,1:T(4,128)(2,1)} %param.24), channel_id=1, source_target_pairs={{0,3},{1,0},{2,1},{3,2},{4,7},{5,4},{6,5},{7,6},{8,11},{9,8},{10,9... | collective-permute-start | bytes 6912008 | tf_op jit(solution)/shard_map/ppermute | solution.py:19
  381.5 23.5 %copy-start.50 = (bf16[2,96,192]{2,1,0:T(8,128)(2,1)S(1)}, bf16[2,96,192]{2,1,0:T(8,128)(2,1)}, u32[]{:S(2)}) copy-start(bf16[2,96,192]{2,1,0:T(8,128)(2,1)} %param.29) | copy-start | bytes 221188
  384.4 296.2 %reduce-scatter.29.cloned.1.call-start = ((), (), s32[]{:S(2)}) async-start(), calls=%async_computation.16 | async-start | bytes 3440640 | tf_op jit(solution)/shard_map/reduce_scatter | solution.py:158
  545.2 10.8 copy-start.30
  623.6 57.0 %copy-start.69 = (f32[768]{0:T(1024)S(1)}, f32[768]{0:T(1024)}, u32[]{:S(2)}) copy-start(f32[768]{0:T(1024)} %get-tuple-element.559) | copy-start | bytes 9220
  627.3 56.1 %copy-start.56 = (f32[768]{0:T(1024)S(1)}, f32[768]{0:T(1024)}, u32[]{:S(2)}) copy-start(f32[768]{0:T(1024)} %get-tuple-element.456) | copy-start | bytes 9220
  627.3 56.1 %copy-start.68 = (f32[768]{0:T(1024)S(1)}, f32[768]{0:T(1024)}, u32[]{:S(2)}) copy-start(f32[768]{0:T(1024)} %get-tuple-element.460) | copy-start | bytes 9220
  627.3 102.1 %all-gather.18.cloned.1.call-start = ((), (), s32[]{:S(2)}) async-start(), calls=%async_computation.18 | async-start | bytes 1327104 | tf_op jit(solution)/shard_map/all_gather | solution.py:131
  627.9 114.2 %all-gather.16.cloned.1.call-start = ((), (), s32[]{:S(2)}) async-start(), calls=%async_computation.17 | async-start | bytes 3440640 | tf_op jit(solution)/shard_map/all_gather | solution.py:154
  684.6 81.9 %all-gather.20.cloned.1.call-start = ((), (), s32[]{:S(2)}) async-start(), calls=%async_computation.19 | async-start | bytes 1327104 | tf_op jit(solution)/shard_map/all_gather | solution.py:132
  685.2 141.7 %reduce-scatter.31.cloned.1.call-start = ((), (), s32[]{:S(2)}) async-start(), calls=%async_computation.20 | async-start | bytes 3440640 | tf_op jit(solution)/shard_map/reduce_scatter | solution.py:158
  772.4 54.4 %copy-start.67 = (f32[768]{0:T(1024)S(1)}, f32[768]{0:T(1024)}, u32[]{:S(2)}) copy-start(f32[768]{0:T(1024)} %get-tuple-element.560) | copy-start | bytes 9220
  772.4 56.5 %copy-start.26 = (bf16[1,448,768]{2,1,0:T(8,128)(2,1)S(1)}, bf16[1,448,768]{2,1,0:T(8,128)(2,1)}, u32[]{:S(2)}) copy-start(bf16[1,448,768]{2,1,0:T(8,128)(2,1)} %param.37) | copy-start | bytes 2064388
  772.5 56.5 %copy-start.55 = (f32[768]{0:T(1024)S(1)}, f32[768]{0:T(1024)}, u32[]{:S(2)}) copy-start(f32[768]{0:T(1024)} %get-tuple-element.455) | copy-start | bytes 9220
  772.5 116.2 %all-gather.22.cloned.1.call-start = ((), (), s32[]{:S(2)}) async-start(), calls=%async_computation.21 | async-start | bytes 3440640 | tf_op jit(solution)/shard_map/all_gather | solution.py:166
  832.2 123.6 %reduce-scatter.33.cloned.1.call-start = ((), (), s32[]{:S(2)}) async-start(), calls=%async_computation.22 | async-start | bytes 3440640 | tf_op jit(solution)/shard_map/reduce_scatter | solution.py:170
  888.6 10.0 copy-start.79
  902.6 56.1 %copy-start.75 = (f32[768]{0:T(1024)S(1)}, f32[768]{0:T(1024)}, u32[]{:S(2)}) copy-start(f32[768]{0:T(1024)} %get-tuple-element.459) | copy-start | bytes 9220
  902.6 116.8 %all-gather.24.cloned.1.call-start = ((), (), s32[]{:S(2)}) async-start(), calls=%async_computation.23 | async-start | bytes 3440640 | tf_op jit(solution)/shard_map/all_gather | solution.py:166
  962.7 174.8 %reduce-scatter.35.cloned.1.call-start = ((), (), s32[]{:S(2)}) async-start(), calls=%async_computation.24 | async-start | bytes 3440640 | tf_op jit(solution)/shard_map/reduce_scatter | solution.py:170
  1081.8 55.7 %copy-start.1 = (bf16[1,448,768]{2,1,0:T(8,128)(2,1)S(1)}, bf16[1,448,768]{2,1,0:T(8,128)(2,1)}, u32[]{:S(2)}) copy-start(bf16[1,448,768]{2,1,0:T(8,128)(2,1)} %param.23) | copy-start | bytes 2064388
  1081.8 55.7 %copy-start.6 = (bf16[1,448,768]{2,1,0:T(8,128)(2,1)S(1)}, bf16[1,448,768]{2,1,0:T(8,128)(2,1)}, u32[]{:S(2)}) copy-start(bf16[1,448,768]{2,1,0:T(8,128)(2,1)} %reduce-scatter.27.cloned.1.call-done) | copy-start | bytes 2064388
  1081.8 55.7 %copy-start.48 = (f32[768]{0:T(1024)S(1)}, f32[768]{0:T(1024)}, u32[]{:S(2)}) copy-start(f32[768]{0:T(1024)} %copy-done.47) | copy-start | bytes 9220
  1081.8 55.7 %copy-start.54 = (f32[768]{0:T(1024)S(1)}, f32[768]{0:T(1024)}, u32[]{:S(2)}) copy-start(f32[768]{0:T(1024)} %copy-done.53) | copy-start | bytes 9220
  1081.8 55.7 %copy-start.60 = (f32[448]{0:T(512)S(1)}, f32[448]{0:T(512)}, u32[]{:S(2)}) copy-start(f32[448]{0:T(512)} %copy-done.59) | copy-start | bytes 5380
  1081.8 55.7 %copy-start.66 = (f32[448]{0:T(512)S(1)}, f32[448]{0:T(512)}, u32[]{:S(2)}) copy-start(f32[448]{0:T(512)} %copy-done.65) | copy-start | bytes 5380
  1084.3 55.2 %copy-start.27 = (f32[1,448,768]{2,1,0:T(8,128)S(1)}, f32[1,448,768]{2,1,0:T(8,128)}, u32[]{:S(2)}) copy-start(f32[1,448,768]{2,1,0:T(8,128)} %get-tuple-element.537) | copy-start | bytes 4128772
  1084.3 181.2 %all-gather.26.cloned.1.call-start = ((), (), s32[]{:S(2)}) async-start(), calls=%async_computation.25 | async-start | bytes 3440640 | tf_op jit(solution)/shard_map/all_gather | solution.py:166
  1142.7 221.0 %reduce-scatter.51.cloned.1.call-start = ((), (), s32[]{:S(2)}) async-start(), calls=%async_computation.33 | async-start | bytes 884736
  1142.7 11.1 copy-start.13
  1166.1 199.2 %reduce-scatter.49.cloned.1.call-start = ((), (), s32[]{:S(2)}) async-start(), calls=%async_computation.32 | async-start | bytes 1327104
  1194.0 422.2 %all-reduce.9.cloned.1.call-start = ((), (), s32[]{:S(2)}) async-start(), calls=%async_computation.34 | async-start | bytes 18432000
  1194.3 10.2 copy-start.16
  1194.4 10.1 copy-start.32
  1265.0 356.5 %reduce-scatter.45.cloned.1.call-start = ((), (), s32[]{:S(2)}) async-start(), calls=%async_computation.30 | async-start | bytes 884736
  1316.8 306.4 %reduce-scatter.43.cloned.1.call-start = ((), (), s32[]{:S(2)}) async-start(), calls=%async_computation.29 | async-start | bytes 2211840
  1337.1 288.0 %reduce-scatter.37.cloned.1.call-start = ((), (), s32[]{:S(2)}) async-start(), calls=%async_computation.26 | async-start | bytes 3440640 | tf_op jit(solution)/shard_map/reduce_scatter | solution.py:170
  1341.9 331.5 %reduce-scatter.39.cloned.1.call-start = ((), (), s32[]{:S(2)}) async-start(), calls=%async_computation.27 | async-start | bytes 2654208 | tf_op jit(solution)/shard_map/reduce_scatter | solution.py:353
  1348.6 8.4 copy-start.71
  1348.6 8.4 copy-start.70
  1348.6 8.4 copy-start.72
  1348.6 8.4 copy-start.78
  1348.7 8.7 copy-start.74
  1348.7 8.7 copy-start.76
  1348.7 8.7 copy-start.73
  1348.7 324.7 %reduce-scatter.41.cloned.1.call-start = ((), (), s32[]{:S(2)}) async-start(), calls=%async_computation.28 | async-start | bytes 2654208 | tf_op jit(solution)/shard_map/reduce_scatter | solution.py:354
  1355.6 317.8 %reduce-scatter.47.cloned.1.call-start = ((), (), s32[]{:S(2)}) async-start(), calls=%async_computation.31 | async-start | bytes 884736
  1367.1 253.5 %copy-start.18 = (bf16[4,448,3,64]{1,3,2,0:T(8,128)(2,1)S(1)}, bf16[4,448,3,64]{1,3,2,0:T(8,128)(2,1)}, u32[]{:S(2)}) copy-start(bf16[4,448,3,64]{1,3,2,0:T(8,128)(2,1)} %get-tuple-element.211) | copy-start | bytes 2064388
  1367.1 253.7 %copy-start.20 = (bf16[4,448,3,64]{1,3,2,0:T(8,128)(2,1)S(1)}, bf16[4,448,3,64]{1,3,2,0:T(8,128)(2,1)}, u32[]{:S(2)}) copy-start(bf16[4,448,3,64]{1,3,2,0:T(8,128)(2,1)} %get-tuple-element.209) | copy-start | bytes 2064388
  (54 other events, 167.2 us)
Sparse Core Ops, SparseCore 0:
  149.2 56.4 all-gather.11
  277.6 96.7 reduce-scatter.26
  384.5 111.7 all-gather.13
  627.4 53.1 reduce-scatter.28
  962.9 56.5 all-gather.23
  1084.5 53.0 reduce-scatter.34
  1265.1 351.0 all-reduce.8
Sparse Core Ops, SparseCore 1:
  629.7 22.6 all-gather.17
  684.7 57.4 all-gather.15
  743.9 22.5 all-gather.19
  772.5 54.3 reduce-scatter.30
  832.2 56.3 all-gather.21
  902.7 53.0 reduce-scatter.32
  1142.7 56.4 all-gather.25
  1202.2 33.6 reduce-scatter.50
  1238.9 36.7 reduce-scatter.48
  1316.8 34.5 reduce-scatter.44
  1354.7 40.1 reduce-scatter.42
  1397.2 120.1 reduce-scatter.36
  1521.1 42.2 reduce-scatter.38
  1567.3 42.2 reduce-scatter.40
  1613.3 35.0 reduce-scatter.46
